TPU v7x, 32 devices: a whole 2x2x4 slice. The times are simulated.
32 devices in a mesh: grp: 4 (over y, x), tile: 8 (over z, core).
Axes of the slice: x: 2, y: 2, z: 4, core: 2. Of those that a mesh axis runs over, the one named last changes fastest.
Arguments:
- observed: bfloat16 [512, 32, 2048], P('tile', 'grp'), as said below
- visible: int32 [32, 2048], P('grp', 'tile'), may hold values from 0 to 65535
- params_start: float32 [8, 32, 2048], P(None, 'grp', 'tile'), may hold values from -1.5 to 1.5, as said below
- light_directions: float32 [3, 32], replicated, may hold values from -1 to 1
- view_dirs: float32 [3, 16], replicated, may hold values from -1 to 1
- gains_start: float32 [32], replicated, may hold values from 0.5 to 1.5
Outputs:
- params_out: float32 [8, 32, 2048], P(None, 'grp', 'tile')
- gains_out: float32 [32], replicated
Inputs may be any that keep to these rules, and one draw needn't show every extreme that they name: `observed`: luminance is positive. `params_start`: tilts within -0.3 to 0.3, diffuse 0.3 to 1.2, specular 0.1 to 0.8, sharpness logit -1.5 to 1.5, ambient -0.2 to 0.3, rim 0 to 0.5, retro -0.3 to 0.3.
All inputs are finite; a program needn't handle non-finite values.
Results may differ from a plain program's by a relative error of at most 0.0003.
Values may be sent and summed in bfloat16 or wider, within the bound.
No kernel may reach another device: no remote copies, remote signals or barrier semaphores. Data moves between devices by JAX's collectives and lax.ppermute only.
A program may use at most 64 MiB of HBM per device.

v0:
```python
import jax
import jax.numpy as jnp
from jax import lax
from jax.sharding import PartitionSpec as P

CAMS = 16
LIGHTS = 32
ITERS = 2
damping = 4.0
lift_z = 1.6


def padded_2(cells, sides, width):
    for axis, dim in sides:
        count = lax.axis_size(axis)
        ends = count - 1
        head = lax.slice_in_dim(cells, 0, width, axis=dim)
        tail = lax.slice_in_dim(cells, cells.shape[dim] - width, cells.shape[dim], axis=dim)
        cells = jnp.concatenate(
            [
                lax.ppermute(tail, axis, [(i, (i + 1) % count) for i in range(ends)]),
                cells,
                lax.ppermute(head, axis, [((i + 1) % count, i) for i in range(ends)]),
            ],
            axis=dim,
        )
    return cells


def unit_columns(raw):
    lifted = raw + jnp.array([0.0, 0.0, lift_z], jnp.float32)[:, None]
    return lifted / jnp.sqrt(jnp.sum(lifted * lifted, axis=0, keepdims=True))


def geometry(light_directions, view_dirs):
    lights = unit_columns(light_directions)
    views = unit_columns(view_dirs)
    raw_half = views.T[:, :, None] + lights[None]
    halves = raw_half / jnp.sqrt(jnp.sum(raw_half * raw_half, axis=1, keepdims=True))
    echoes = jnp.sum(views.T[:, :, None] * lights[None], axis=1)
    return (lights, halves, views.T, echoes)


def facing(dir_x, dir_y, dir_z, tilt_u, tilt_v, scale_q):
    facing_dot = (dir_x * tilt_u + dir_y * tilt_v + dir_z) * scale_q
    by_u = (dir_x - facing_dot * tilt_u * scale_q) * scale_q
    by_v = (dir_y - facing_dot * tilt_v * scale_q) * scale_q
    return (facing_dot, by_u, by_v)


def camera_terms(observed_c, weight_c, params, gains, lights, half_c, view_c, echo_c):
    tilt_u, tilt_v, diffuse, specular, sharp_raw, ambient, rim_gain, retro_gain = [
        params[i] for i in range(8)
    ]
    scale_q = 1.0 / jnp.sqrt(1.0 + tilt_u * tilt_u + tilt_v * tilt_v)
    light_dot, light_u, light_v = facing(
        lights[0][:, None], lights[1][:, None], lights[2][:, None], tilt_u, tilt_v, scale_q
    )
    half_dot, half_u, half_v = facing(
        half_c[0][:, None], half_c[1][:, None], half_c[2][:, None], tilt_u, tilt_v, scale_q
    )
    view_dot, view_u, view_v = facing(view_c[0], view_c[1], view_c[2], tilt_u, tilt_v, scale_q)
    sigma = jax.nn.sigmoid(sharp_raw)
    sharp = 1.0 + 20.0 * sigma
    lobe = jnp.exp(sharp * (half_dot - 1.0))
    back = 1.0 - view_dot
    rim_shape = back * back
    shaped = (
        diffuse * light_dot
        + specular * lobe
        + ambient
        + rim_gain * rim_shape
        + retro_gain * echo_c[:, None]
    )
    full = light_dot.shape
    jacob = [
        diffuse * light_u + specular * sharp * lobe * half_u - 2.0 * rim_gain * back * view_u,
        diffuse * light_v + specular * sharp * lobe * half_v - 2.0 * rim_gain * back * view_v,
        light_dot,
        lobe,
        specular * lobe * (half_dot - 1.0) * 20.0 * sigma * (1.0 - sigma),
        jnp.ones(full, jnp.float32),
        jnp.broadcast_to(rim_shape, full),
        jnp.broadcast_to(echo_c[:, None], full),
    ]
    column = gains[:, None]
    resid = observed_c.astype(jnp.float32) - column * shaped
    scaled = [column * piece for piece in jacob]
    surface_normal = []
    for i in range(8):
        for j in range(i, 8):
            surface_normal.append(weight_c * jnp.sum(scaled[i] * scaled[j], axis=0))
    right_side = [weight_c * jnp.sum(piece * resid, axis=0) for piece in scaled]
    lifted = jnp.sum(weight_c * shaped * resid, axis=1)
    energy = jnp.sum(weight_c * shaped * shaped, axis=1)
    return (jnp.stack(surface_normal), jnp.stack(right_side), lifted, energy)


def assemble(observed, weights, params, gains, lights, halves, views, echoes):
    texels = params.shape[1]

    def one_camera(carry, inputs):
        observed_c, weight_c, half_c, view_c, echo_c = inputs
        terms = camera_terms(observed_c, weight_c, params, gains, lights, half_c, view_c, echo_c)
        return (tuple((a + b for a, b in zip(carry, terms))), None)

    start = (
        jnp.zeros((36, texels), jnp.float32),
        jnp.zeros((8, texels), jnp.float32),
        jnp.zeros((LIGHTS,), jnp.float32),
        jnp.zeros((LIGHTS,), jnp.float32),
    )
    result, unused = lax.scan(one_camera, start, (observed, weights, halves, views, echoes))
    return result


def solve_eight(surface_normal, right_side):
    entries = {}
    where = 0
    for i in range(8):
        for j in range(i, 8):
            entries[i, j] = surface_normal[where]
            where += 1
    lower = {}
    for j in range(8):
        accum = entries[j, j] + damping
        for k in range(j):
            accum = accum - lower[j, k] * lower[j, k]
        root = jnp.sqrt(accum)
        lower[j, j] = root
        for i in range(j + 1, 8):
            accum = entries[j, i]
            for k in range(j):
                accum = accum - lower[i, k] * lower[j, k]
            lower[i, j] = accum / root
    forward = []
    for i in range(8):
        accum = right_side[i]
        for k in range(i):
            accum = accum - lower[i, k] * forward[k]
        forward.append(accum / lower[i, i])
    answer = [None] * 8
    for i in range(7, -1, -1):
        accum = forward[i]
        for k in range(i + 1, 8):
            accum = accum - lower[k, i] * answer[k]
        answer[i] = accum / lower[i, i]
    return jnp.stack(answer)


def smooth_tilts(tilt):
    rows = tilt.shape[1]
    cols = tilt.shape[2]
    padded = padded_2(tilt, (("grp", 1), ("tile", 2)), 1)
    boxed = jnp.zeros(tilt.shape, jnp.float32)
    for i in range(3):
        for j in range(3):
            boxed = boxed + padded[:, i : i + rows, j : j + cols]
    return 0.5 * tilt + boxed * (0.5 / 9.0)


def update_gains(gains, lifted, energy):
    totals = lax.psum(jnp.stack([lifted, energy]), ("grp", "tile"))
    return gains + totals[0] / (totals[1] + 1.0)


def on_device(observed, visible, params_start, light_directions, view_dirs, gains_start):
    lights, halves, views, echoes = geometry(light_directions, view_dirs)
    rows = visible.shape[0]
    cols = visible.shape[1]
    shifts = jnp.arange(CAMS, dtype=jnp.int32)
    weights = jnp.bitwise_and(jnp.right_shift(visible.reshape(1, -1), shifts[:, None]), 1).astype(
        jnp.float32
    )
    params = params_start.reshape(8, -1)
    gains = gains_start
    regrouped = lax.all_to_all(observed, "tile", split_axis=2, concat_axis=0, tiled=True)
    flat_obs = regrouped.reshape(CAMS, LIGHTS, rows * cols)
    first_terms = assemble(flat_obs, weights, params, gains, lights, halves, views, echoes)
    for iteration in range(ITERS):
        if iteration == 0:
            surface_normal, right_side, lifted, energy = first_terms
        else:
            surface_normal, right_side, lifted, energy = assemble(
                flat_obs, weights, params, gains, lights, halves, views, echoes
            )
        params = params + solve_eight(surface_normal, right_side)
        gains = update_gains(gains, lifted, energy)
        grid = params.reshape(8, rows, cols)
        params = jnp.concatenate([smooth_tilts(grid[:2]), grid[2:]], axis=0).reshape(8, -1)
    return (params.reshape(8, rows, cols), gains)


def solution(mesh):
    return jax.shard_map(
        on_device,
        mesh=mesh,
        in_specs=(P("tile", "grp", None), P("grp", "tile"), P(None, "grp", "tile"), P(), P(), P()),
        out_specs=(P(None, "grp", "tile"), P()),
        check_vma=False,
    )
```

profile of v0, /device:TPU:3, one launch (start us, length us, event | category | flops | bytes accessed | tf_op | source)
XLA Modules:
  0.0 603.4 jit_solution(8106772559715947173)
XLA Ops:
  0.6 6.7 %copy.16 = bf16[64,8,2048]{0,1,2:T(8,128)(2,1)} copy(bf16[64,8,2048]{2,1,0:T(8,128)(2,1)} %param.12) | data formatting | bytes 4194304 | tf_op args[0]
  7.3 7.6 %reshape.750 = bf16[8,2,65536]{2,1,0:T(2,128)(2,1)} reshape(bf16[2048,8,64]{2,1,0:T(8,128)(2,1)} %bitcast.458) | data formatting | bytes 4194304
  14.9 5.7 all-to-all-start
  22.1 46.7 %all-to-all-done = bf16[8,2,65536]{2,1,0:T(2,128)(2,1)S(1)} async-done(((bf16[8,2,65536]{2,1,0:T(2,128)(2,1)}), bf16[8,2,65536]{2,1,0:T(2,128)(2,1)S(1)}, u32[]{:S(2)}, u32[]{:S(2)}) %all-to-all-start) | async-done | bytes 2097184 | tf_op jit(solution)/shard_map/all_to_all | solution.py:177
  68.8 5.0 reshape.751
  73.8 5.0 copy.17
  81.2 201.9 %while.40 = (s32[]{:T(128)}, f32[36,2048]{1,0:T(8,128)S(1)}, f32[8,2048]{1,0:T(8,128)S(1)}, f32[32]{0:T(128)S(1)}, f32[32]{0:T(128)S(1)}, /*index=5*/f32[16,2048...) while((s32[]{:T(128)}, f32[36,2048]{1,0:T(8,128)S(1)}, ...), condition=%wide.region_51.52_spmd.clone, body=%wide.region_5.51_spmd.clone.sunk | while | flops 14035169 | bytes 4423358 | solution.py:113
  82.5 2.4 multiply_multiply_fusion.36
  95.1 2.4 multiply_multiply_fusion.36
  107.8 2.4 multiply_multiply_fusion.36
  120.4 2.4 multiply_multiply_fusion.36
  133.0 2.4 multiply_multiply_fusion.36
  145.6 2.4 multiply_multiply_fusion.36
  158.2 2.4 multiply_multiply_fusion.36
  170.8 2.4 multiply_multiply_fusion.36
  183.5 2.4 multiply_multiply_fusion.36
  196.1 2.4 multiply_multiply_fusion.36
  208.7 2.4 multiply_multiply_fusion.36
  221.3 2.4 multiply_multiply_fusion.36
  233.9 2.4 multiply_multiply_fusion.36
  246.5 2.4 multiply_multiply_fusion.36
  259.2 2.4 multiply_multiply_fusion.36
  271.8 2.4 multiply_multiply_fusion.36
  284.9 3.1 collective-permute-start
  290.2 38.6 %psum.14 = f32[2,32]{1,0:T(2,128)S(1)} all-reduce(f32[2,32]{1,0:T(2,128)S(1)} %pad_maximum_fusion.10), channel_id=1, replica_groups=mesh['grp'=4,'tile'=8] {'grp','tile'}, use_global_device_ids=true, to_apply=%region_52.53 | all-reduce | flops 64 | bytes 512 | tf_op jit(solution)/shard_map/psum | solution.py:163
  329.5 5.9 collective-permute-start.2
  337.5 2.9 collective-permute-done.3
  340.8 203.1 %while.41 = (s32[]{:T(128)}, f32[36,2048]{1,0:T(8,128)S(1)}, f32[8,2048]{1,0:T(8,128)S(1)}, f32[32]{0:T(128)S(1)}, f32[32]{0:T(128)S(1)}, /*index=5*/f32[16,2048...) while((s32[]{:T(128)}, f32[36,2048]{1,0:T(8,128)S(1)}, ...), condition=%wide.region_100.101_spmd.clone, body=%wide.region_54.100_spmd.clone.sunk | while | flops 14035169 | bytes 4423358 | solution.py:113
  342.1 2.4 multiply_multiply_fusion.38
  354.8 2.4 multiply_multiply_fusion.38
  367.5 2.4 multiply_multiply_fusion.38
  380.2 2.4 multiply_multiply_fusion.38
  392.8 2.4 multiply_multiply_fusion.38
  405.5 2.4 multiply_multiply_fusion.38
  418.2 2.4 multiply_multiply_fusion.38
  430.9 2.4 multiply_multiply_fusion.38
  443.6 2.4 multiply_multiply_fusion.38
  456.3 2.4 multiply_multiply_fusion.38
  469.0 2.4 multiply_multiply_fusion.38
  481.7 2.4 multiply_multiply_fusion.38
  494.4 2.4 multiply_multiply_fusion.38
  519.8 2.4 multiply_multiply_fusion.38
  532.5 2.4 multiply_multiply_fusion.38
  543.9 37.7 %psum.15 = f32[2,32]{1,0:T(2,128)S(1)} all-reduce(f32[2,32]{1,0:T(2,128)S(1)} %pad_maximum_fusion.11), channel_id=1, replica_groups=mesh['grp'=4,'tile'=8] {'grp','tile'}, use_global_device_ids=true, to_apply=%region_101.102 | all-reduce | flops 64 | bytes 512 | tf_op jit(solution)/shard_map/psum | solution.py:163
  583.3 3.1 collective-permute-start.4
  589.2 2.5 collective-permute-done.5
  591.7 5.8 collective-permute-start.6
  599.5 3.1 collective-permute-done.7
  (827 shorter events, 342.5 us)
Async XLA Ops:
  14.9 5.8 copy-start.3
  14.9 5.8 copy-start.5
  14.9 6.0 %copy-start.4 = (f32[3,32]{1,0:T(4,128)S(1)}, f32[3,32]{1,0:T(4,128)}, u32[]{:S(2)}) copy-start(f32[3,32]{1,0:T(4,128)} %param.15) | copy-start | bytes 1156
  14.9 6.4 %copy-start.1 = (f32[8,8,256]{2,1,0:T(8,128)S(1)}, f32[8,8,256]{2,1,0:T(8,128)}, u32[]{:S(2)}) copy-start(f32[8,8,256]{2,1,0:T(8,128)} %param.14) | copy-start | bytes 196612
  14.9 6.5 %copy-start.2 = (s32[8,256]{1,0:T(8,128)S(1)}, s32[8,256]{1,0:T(8,128)}, u32[]{:S(2)}) copy-start(s32[8,256]{1,0:T(8,128)} %param.13) | copy-start | bytes 24580
  14.9 6.5 %copy-start = (f32[32]{0:T(128)S(1)}, f32[32]{0:T(128)}, u32[]{:S(2)}) copy-start(f32[32]{0:T(128)} %param.17) | copy-start | bytes 388
  14.9 53.9 %all-to-all-start = ((bf16[8,2,65536]{2,1,0:T(2,128)(2,1)}), bf16[8,2,65536]{2,1,0:T(2,128)(2,1)S(1)}, u32[]{:S(2)}, u32[]{:S(2)}) async-start(bf16[8,2,65536]{2,1,0:T(2,128)(2,1)} %reshape.750), calls=%async_computation | async-start | bytes 4194304 | tf_op jit(solution)/shard_map/all_to_all | solution.py:177
  284.9 44.5 %collective-permute-start = (f32[2,1,256]{2,1,0:T(1,128)S(1)}, f32[2,1,256]{2,1,0:T(1,128)S(1)}, u32[]{:S(2)}, u32[]{:S(2)}) collective-permute-start(f32[2,1,256]{2,1,0:T(1,128)S(1)} %get-tuple-element.1093), channel_id=1, source_target_pairs={{0,8},{8,16},{16,24},{1,9},{9,17},{17,25},{2,10},{10,18},{18,26},{... | collective-permute-start | bytes 6152 | tf_op jit(solution)/shard_map/ppermute | solution.py:21
  288.0 41.4 %collective-permute-start.1 = (f32[2,1,256]{2,1,0:T(1,128)S(1)}, f32[2,1,256]{2,1,0:T(1,128)S(1)}, u32[]{:S(2)}, u32[]{:S(2)}) collective-permute-start(f32[2,1,256]{2,1,0:T(1,128)S(1)} %get-tuple-element.1094), channel_id=1, source_target_pairs={{8,0},{16,8},{24,16},{9,1},{17,9},{25,17},{10,2},{18,10},{26,18},{... | collective-permute-start | bytes 6152 | tf_op jit(solution)/shard_map/ppermute | solution.py:23
  329.5 8.0 %collective-permute-start.2 = (f32[2,10,1]{2,1,0:T(8,128)S(1)}, f32[2,10,1]{2,1,0:T(8,128)S(1)}, u32[]{:S(2)}, u32[]{:S(2)}) collective-permute-start(f32[2,10,1]{2,1,0:T(8,128)S(1)} %get-tuple-element.1081), channel_id=1, source_target_pairs={{0,1},{1,2},{2,3},{3,4},{4,5},{5,6},{6,7},{8,9},{9,10},{10,11},{11... | collective-permute-start | bytes 248 | tf_op jit(solution)/shard_map/ppermute | solution.py:21
  335.4 5.1 collective-permute-start.3
  583.3 5.9 collective-permute-start.4
  586.4 5.2 collective-permute-start.5
  591.7 7.8 %collective-permute-start.6 = (f32[2,10,1]{2,1,0:T(8,128)S(1)}, f32[2,10,1]{2,1,0:T(8,128)S(1)}, u32[]{:S(2)}, u32[]{:S(2)}) collective-permute-start(f32[2,10,1]{2,1,0:T(8,128)S(1)} %get-tuple-element.1079), channel_id=1, source_target_pairs={{0,1},{1,2},{2,3},{3,4},{4,5},{5,6},{6,7},{8,9},{9,10},{10,11},{11... | collective-permute-start | bytes 248 | tf_op jit(solution)/shard_map/ppermute | solution.py:21
  597.6 5.1 collective-permute-start.7
where the time goes:
time: 608 us; the launch traced here: 603 us
  other arithmetic  366 us (60%)
  blocking collectives  76.3 us (13%)
  local copies, waits for them, and re-layouts  67.8 us (11%)
  waiting for transfers between devices  55.2 us (9%)
  starting transfers between devices  32 us (5%)
    mul x32, other arithmetic, camera_terms(): 2.0 * rim_gain * back * view_v  78.1 us
    psum x2, blocking collectives, update_gains(): totals = lax.psum(jnp.stack([lifted, energy]), ('grp', 'tile'))  76.3 us
    reduce_sum x98, other arithmetic, camera_terms(): surface_normal.append(weight_c * jnp.sum(scaled[i] * scaled[j], axis=0))  61.1 us
    mul x32, other arithmetic, camera_terms(): rim_shape = back * back  57.2 us
    all_to_all x1, waiting for transfers between devices, on_device(): lax.all_to_all(observed, 'tile', split_axis=2, concat_axis=0, tiled=True)  46.7 us
    reduce_sum x32, other arithmetic, camera_terms(): lifted = jnp.sum(weight_c * shaped * resid, axis=1)  46.1 us
    mul x32, other arithmetic, camera_terms(): right_side = [weight_c * jnp.sum(piece * resid, axis=0) for piece in scaled]  43.2 us
    reduce_sum x32, other arithmetic, camera_terms(): right_side = [weight_c * jnp.sum(piece * resid, axis=0) for piece in scaled]  41.6 us
  transfers between devices with their start and end apart: 9, of which 4 were waited for; matrix products, arithmetic and copies ran while one was open for 0% of the time, Pallas kernels for 0%

commit v1 on v0

--- a/solution.py
+++ b/solution.py
@@ -8,6 +8,22 @@
 ITERS = 2
 damping = 4.0
 lift_z = 1.6
+
+
+def exchange_in_pairs(x, axis, split, join):
+    ways, here = (lax.axis_size(axis), lax.axis_index(axis))
+    width = x.shape[split] // ways
+    lengths = list(x.shape)
+    lengths[split] = width
+    height = lengths[join]
+    lengths[join] = height * ways
+    full = jnp.zeros(lengths, x.dtype)
+    for mask in range(ways):
+        part = lax.dynamic_slice_in_dim(x, (here ^ mask) * width, width, axis=split)
+        if mask:
+            part = lax.ppermute(part, axis, [(d, d ^ mask) for d in range(ways)])
+        full = lax.dynamic_update_slice_in_dim(full, part, (here ^ mask) * height, axis=join)
+    return full
 
 
 def padded_2(cells, sides, width):
@@ -174,7 +190,7 @@
     )
     params = params_start.reshape(8, -1)
     gains = gains_start
-    regrouped = lax.all_to_all(observed, "tile", split_axis=2, concat_axis=0, tiled=True)
+    regrouped = exchange_in_pairs(observed, "tile", 2, 0)
     flat_obs = regrouped.reshape(CAMS, LIGHTS, rows * cols)
     first_terms = assemble(flat_obs, weights, params, gains, lights, halves, views, echoes)
     for iteration in range(ITERS):

time: 608 us -> 587 us (0.965)
  waiting for transfers between devices: 55.2 us -> 30.5 us
  local copies, waits for them, and re-layouts: 67.8 us -> 51.3 us
  blocking collectives: 76.3 us -> 89.6 us
    all_to_all x1 -> x0, waiting for transfers between devices: 46.7 us -> none  [on_device(): lax.all_to_all(observed, 'tile', split_axis=2, concat_axis=0, tiled=True)]
    ppermute x0 -> x7, waiting for transfers between devices: none -> 24.2 us  [exchange_in_pairs(): part = lax.ppermute(part, axis, [(d, d ^ mask) for d in range(ways)])]
    unnamed x30 -> x29, local copies, waits for them, and re-layouts: 19.4 us -> 1.6 us
    psum x2, blocking collectives: 76.3 us -> 89.6 us  [update_gains(): totals = lax.psum(jnp.stack([lifted, energy]), ('grp', 'tile'))]
    ppermute x0 -> x7, starting transfers between devices: none -> 10.7 us  [exchange_in_pairs(): part = lax.ppermute(part, axis, [(d, d ^ mask) for d in range(ways)])]
  transfers between devices with their start and end apart: 9 -> 15, of which waited for: 4 -> 6; matrix products, arithmetic and copies ran while one was open for 0% -> 1% of each run, Pallas kernels for 0% -> 0%
where the time goes in v1:
time: 587 us; the launch traced here: 582 us
  other arithmetic  369 us (63%)
  blocking collectives  89.6 us (15%)
  local copies, waits for them, and re-layouts  51.3 us (9%)
  starting transfers between devices  35.6 us (6%)
  waiting for transfers between devices  30.5 us (5%)
    psum x2, blocking collectives, update_gains(): totals = lax.psum(jnp.stack([lifted, energy]), ('grp', 'tile'))  89.6 us
    mul x32, other arithmetic, camera_terms(): 2.0 * rim_gain * back * view_v  78.2 us
    reduce_sum x98, other arithmetic, camera_terms(): surface_normal.append(weight_c * jnp.sum(scaled[i] * scaled[j], axis=0))  61.4 us
    mul x32, other arithmetic, camera_terms(): rim_shape = back * back  57.2 us
    reduce_sum x32, other arithmetic, camera_terms(): lifted = jnp.sum(weight_c * shaped * resid, axis=1)  46.3 us
    mul x32, other arithmetic, camera_terms(): right_side = [weight_c * jnp.sum(piece * resid, axis=0) for piece in scaled]  44.8 us
    reduce_sum x32, other arithmetic, camera_terms(): right_side = [weight_c * jnp.sum(piece * resid, axis=0) for piece in scaled]  42.4 us
    ppermute x7, waiting for transfers between devices, exchange_in_pairs(): part = lax.ppermute(part, axis, [(d, d ^ mask) for d in range(ways)])  24.2 us
  transfers between devices with their start and end apart: 15, of which 6 were waited for; matrix products, arithmetic and copies ran while one was open for 1% of the time, Pallas kernels for 0%

profile of v1, /device:TPU:3, one launch (start us, length us, event | category | flops | bytes accessed | tf_op | source)
XLA Modules:
  0.0 582.0 jit_solution(6742043659297808587)
XLA Ops:
  10.3 3.4 collective-permute-start.5
  14.6 8.6 %collective-permute-done.1 = bf16[64,8,256]{2,1,0:T(8,128)(2,1)} collective-permute-done((bf16[64,8,256]{2,1,0:T(8,128)(2,1)}, bf16[64,8,256]{2,1,0:T(8,128)(2,1)}, u32[]{:S(2)}, u32[]{:S(2)}) %collective-permute-start.1) | collective-permute-done | bytes 262176 | tf_op jit(solution)/shard_map/ppermute | solution.py:24
  26.4 2.5 collective-permute-done.2
  30.9 13.0 %collective-permute-done.4 = bf16[64,8,256]{2,1,0:T(8,128)(2,1)} collective-permute-done((bf16[64,8,256]{2,1,0:T(8,128)(2,1)}, bf16[64,8,256]{2,1,0:T(8,128)(2,1)}, u32[]{:S(2)}, u32[]{:S(2)}) %collective-permute-start.4) | collective-permute-done | bytes 262176 | tf_op jit(solution)/shard_map/ppermute | solution.py:24
  45.0 2.4 reshape.744
  47.4 204.0 %while.40 = (s32[]{:T(128)}, f32[36,2048]{1,0:T(8,128)S(1)}, f32[8,2048]{1,0:T(8,128)S(1)}, f32[32]{0:T(128)S(1)}, f32[32]{0:T(128)S(1)}, /*index=5*/f32[16,2048...) while((s32[]{:T(128)}, f32[36,2048]{1,0:T(8,128)S(1)}, ...), condition=%wide.region_51.52_spmd.clone, body=%wide.region_5.51_spmd.clone.sunk | while | flops 14035169 | bytes 4423358 | solution.py:129
  48.7 2.4 multiply_multiply_fusion.36
  61.4 2.4 multiply_multiply_fusion.36
  74.2 2.4 multiply_multiply_fusion.36
  86.9 2.4 multiply_multiply_fusion.36
  99.7 2.4 multiply_multiply_fusion.36
  112.4 2.4 multiply_multiply_fusion.36
  125.2 2.4 multiply_multiply_fusion.36
  137.9 2.4 multiply_multiply_fusion.36
  150.7 2.4 multiply_multiply_fusion.36
  163.4 2.4 multiply_multiply_fusion.36
  176.2 2.4 multiply_multiply_fusion.36
  188.9 2.4 multiply_multiply_fusion.36
  201.7 2.4 multiply_multiply_fusion.36
  214.4 2.4 multiply_multiply_fusion.36
  227.2 2.4 multiply_multiply_fusion.36
  239.9 2.4 multiply_multiply_fusion.36
  253.2 3.1 collective-permute-start.7
  258.5 49.9 %psum.14 = f32[2,32]{1,0:T(2,128)S(1)} all-reduce(f32[2,32]{1,0:T(2,128)S(1)} %pad_maximum_fusion.10), channel_id=1, replica_groups=mesh['grp'=4,'tile'=8] {'grp','tile'}, use_global_device_ids=true, to_apply=%region_52.53 | all-reduce | flops 64 | bytes 512 | tf_op jit(solution)/shard_map/psum | solution.py:179
  309.1 3.4 collective-permute-start.10
  312.5 2.3 collective-permute-start.9
  315.9 203.6 %while.41 = (s32[]{:T(128)}, f32[36,2048]{1,0:T(8,128)S(1)}, f32[8,2048]{1,0:T(8,128)S(1)}, f32[32]{0:T(128)S(1)}, f32[32]{0:T(128)S(1)}, /*index=5*/f32[16,2048...) while((s32[]{:T(128)}, f32[36,2048]{1,0:T(8,128)S(1)}, ...), condition=%wide.region_100.101_spmd.clone, body=%wide.region_54.100_spmd.clone.sunk | while | flops 14035169 | bytes 4423358 | solution.py:129
  317.2 2.4 multiply_multiply_fusion.38
  330.0 2.4 multiply_multiply_fusion.38
  342.7 2.4 multiply_multiply_fusion.38
  355.4 2.4 multiply_multiply_fusion.38
  368.1 2.4 multiply_multiply_fusion.38
  380.9 2.4 multiply_multiply_fusion.38
  393.6 2.4 multiply_multiply_fusion.38
  406.3 2.4 multiply_multiply_fusion.38
  419.1 2.4 multiply_multiply_fusion.38
  431.8 2.4 multiply_multiply_fusion.38
  444.5 2.4 multiply_multiply_fusion.38
  457.2 2.4 multiply_multiply_fusion.38
  470.0 2.4 multiply_multiply_fusion.38
  482.7 2.4 multiply_multiply_fusion.38
  495.4 2.4 multiply_multiply_fusion.38
  508.1 2.4 multiply_multiply_fusion.38
  519.6 39.7 %psum.15 = f32[2,32]{1,0:T(2,128)S(1)} all-reduce(f32[2,32]{1,0:T(2,128)S(1)} %pad_maximum_fusion.11), channel_id=1, replica_groups=mesh['grp'=4,'tile'=8] {'grp','tile'}, use_global_device_ids=true, to_apply=%region_101.102 | all-reduce | flops 64 | bytes 512 | tf_op jit(solution)/shard_map/psum | solution.py:179
  561.0 3.1 collective-permute-start.11
  566.9 2.5 collective-permute-done.12
  569.4 6.7 %collective-permute-start.13 = (f32[2,10,1]{2,1,0:T(8,128)S(1)}, f32[2,10,1]{2,1,0:T(8,128)S(1)}, u32[]{:S(2)}, u32[]{:S(2)}) collective-permute-start(f32[2,10,1]{2,1,0:T(8,128)S(1)} %get-tuple-element.1087), channel_id=1, source_target_pairs={{0,1},{1,2},{2,3},{3,4},{4,5},{5,6},{6,7},{8,9},{9,10},{10,11},{11... | collective-permute-start | bytes 248 | tf_op jit(solution)/shard_map/ppermute | solution.py:37
  578.1 3.1 collective-permute-done.14
  (846 shorter events, 354.2 us)
Async XLA Ops:
  0.7 1.6 copy-start
  2.3 6.4 %copy-start.4 = (f32[3,16]{1,0:T(4,128)S(1)}, f32[3,16]{1,0:T(4,128)}, u32[]{:S(2)}) copy-start(f32[3,16]{1,0:T(4,128)} %param.16) | copy-start | bytes 580
  2.3 6.4 %copy-start.6 = (f32[3]{0:T(128)S(1)}, f32[3]{0:T(128)}, u32[]{:S(2)}) copy-start(f32[3]{0:T(128)} %constant.155.clone) | copy-start | bytes 40
  2.3 6.7 %copy-start.5 = (f32[3,32]{1,0:T(4,128)S(1)}, f32[3,32]{1,0:T(4,128)}, u32[]{:S(2)}) copy-start(f32[3,32]{1,0:T(4,128)} %param.15) | copy-start | bytes 1156
  2.3 7.1 %copy-start.3 = (s32[8,256]{1,0:T(8,128)S(1)}, s32[8,256]{1,0:T(8,128)}, u32[]{:S(2)}) copy-start(s32[8,256]{1,0:T(8,128)} %param.13) | copy-start | bytes 24580
  2.3 7.1 %copy-start.2 = (f32[8,8,256]{2,1,0:T(8,128)S(1)}, f32[8,8,256]{2,1,0:T(8,128)}, u32[]{:S(2)}) copy-start(f32[8,8,256]{2,1,0:T(8,128)} %param.14) | copy-start | bytes 196612
  2.3 7.1 %copy-start.1 = (f32[32]{0:T(128)S(1)}, f32[32]{0:T(128)}, u32[]{:S(2)}) copy-start(f32[32]{0:T(128)} %param.17) | copy-start | bytes 388
  3.6 6.6 %collective-permute-start = (bf16[64,8,256]{2,1,0:T(8,128)(2,1)}, bf16[64,8,256]{2,1,0:T(8,128)(2,1)}, u32[]{:S(2)}, u32[]{:S(2)}) collective-permute-start(bf16[64,8,256]{2,1,0:T(8,128)(2,1)} %get-tuple-element.1079), channel_id=1, source_target_pairs={{0,1},{1,0},{2,3},{3,2},{4,5},{5,4},{6,7},{7,6},{8,9},{9,8},{10,11... | collective-permute-start | bytes 786440 | tf_op jit(solution)/shard_map/ppermute | solution.py:24
  4.3 18.9 %collective-permute-start.1 = (bf16[64,8,256]{2,1,0:T(8,128)(2,1)}, bf16[64,8,256]{2,1,0:T(8,128)(2,1)}, u32[]{:S(2)}, u32[]{:S(2)}) collective-permute-start(bf16[64,8,256]{2,1,0:T(8,128)(2,1)} %get-tuple-element.1078), channel_id=1, source_target_pairs={{0,2},{1,3},{2,0},{3,1},{4,6},{5,7},{6,4},{7,5},{8,10},{9,11},{10,... | collective-permute-start | bytes 786440 | tf_op jit(solution)/shard_map/ppermute | solution.py:24
  5.6 23.4 %collective-permute-start.2 = (bf16[64,8,256]{2,1,0:T(8,128)(2,1)}, bf16[64,8,256]{2,1,0:T(8,128)(2,1)}, u32[]{:S(2)}, u32[]{:S(2)}) collective-permute-start(bf16[64,8,256]{2,1,0:T(8,128)(2,1)} %get-tuple-element.1077), channel_id=1, source_target_pairs={{0,3},{1,2},{2,1},{3,0},{4,7},{5,6},{6,5},{7,4},{8,11},{9,10},{10,... | collective-permute-start | bytes 786440 | tf_op jit(solution)/shard_map/ppermute | solution.py:24
  5.9 24.0 %collective-permute-start.3 = (bf16[64,8,256]{2,1,0:T(8,128)(2,1)}, bf16[64,8,256]{2,1,0:T(8,128)(2,1)}, u32[]{:S(2)}, u32[]{:S(2)}) collective-permute-start(bf16[64,8,256]{2,1,0:T(8,128)(2,1)} %get-tuple-element.1076), channel_id=1, source_target_pairs={{0,4},{1,5},{2,6},{3,7},{4,0},{5,1},{6,2},{7,3},{8,12},{9,13},{10,... | collective-permute-start | bytes 786440 | tf_op jit(solution)/shard_map/ppermute | solution.py:24
  8.2 35.7 %collective-permute-start.4 = (bf16[64,8,256]{2,1,0:T(8,128)(2,1)}, bf16[64,8,256]{2,1,0:T(8,128)(2,1)}, u32[]{:S(2)}, u32[]{:S(2)}) collective-permute-start(bf16[64,8,256]{2,1,0:T(8,128)(2,1)} %get-tuple-element.1075), channel_id=1, source_target_pairs={{0,5},{1,4},{2,7},{3,6},{4,1},{5,0},{6,3},{7,2},{8,13},{9,12},{10,... | collective-permute-start | bytes 786440 | tf_op jit(solution)/shard_map/ppermute | solution.py:24
  10.3 34.7 %collective-permute-start.5 = (bf16[64,8,256]{2,1,0:T(8,128)(2,1)}, bf16[64,8,256]{2,1,0:T(8,128)(2,1)S(1)}, u32[]{:S(2)}, u32[]{:S(2)}) collective-permute-start(bf16[64,8,256]{2,1,0:T(8,128)(2,1)} %get-tuple-element.1081), channel_id=1, source_target_pairs={{0,6},{1,7},{2,4},{3,5},{4,2},{5,3},{6,0},{7,1},{8,14},{9,15},{10,... | collective-permute-start | bytes 786440 | tf_op jit(solution)/shard_map/ppermute | solution.py:24
  23.2 21.7 %collective-permute-start.6 = (bf16[64,8,256]{2,1,0:T(8,128)(2,1)S(1)}, bf16[64,8,256]{2,1,0:T(8,128)(2,1)S(1)}, u32[]{:S(2)}, u32[]{:S(2)}) collective-permute-start(bf16[64,8,256]{2,1,0:T(8,128)(2,1)S(1)} %get-tuple-element.1074), channel_id=1, source_target_pairs={{0,7},{1,6},{2,5},{3,4},{4,3},{5,2},{6,1},{7,0},{8,15},{9,14},{10,... | collective-permute-start | bytes 786440 | tf_op jit(solution)/shard_map/ppermute | solution.py:24
  253.2 55.9 %collective-permute-start.7 = (f32[2,1,256]{2,1,0:T(1,128)S(1)}, f32[2,1,256]{2,1,0:T(1,128)S(1)}, u32[]{:S(2)}, u32[]{:S(2)}) collective-permute-start(f32[2,1,256]{2,1,0:T(1,128)S(1)} %get-tuple-element.1101), channel_id=1, source_target_pairs={{0,8},{8,16},{16,24},{1,9},{9,17},{17,25},{2,10},{10,18},{18,26},{... | collective-permute-start | bytes 6152 | tf_op jit(solution)/shard_map/ppermute | solution.py:37
  256.3 52.7 %collective-permute-start.8 = (f32[2,1,256]{2,1,0:T(1,128)S(1)}, f32[2,1,256]{2,1,0:T(1,128)S(1)}, u32[]{:S(2)}, u32[]{:S(2)}) collective-permute-start(f32[2,1,256]{2,1,0:T(1,128)S(1)} %get-tuple-element.1102), channel_id=1, source_target_pairs={{8,0},{16,8},{24,16},{9,1},{17,9},{25,17},{10,2},{18,10},{26,18},{... | collective-permute-start | bytes 6152 | tf_op jit(solution)/shard_map/ppermute | solution.py:39
  309.1 5.8 collective-permute-start.10
  312.5 3.1 collective-permute-start.9
  561.0 5.9 %collective-permute-start.11 = (f32[2,1,256]{2,1,0:T(1,128)S(1)}, f32[2,1,256]{2,1,0:T(1,128)S(1)}, u32[]{:S(2)}, u32[]{:S(2)}) collective-permute-start(f32[2,1,256]{2,1,0:T(1,128)S(1)} %get-tuple-element.1095), channel_id=1, source_target_pairs={{0,8},{8,16},{16,24},{1,9},{9,17},{17,25},{2,10},{10,18},{18,26},{... | collective-permute-start | bytes 6152 | tf_op jit(solution)/shard_map/ppermute | solution.py:37
  564.1 5.2 collective-permute-start.12
  569.4 8.7 %collective-permute-start.13 = (f32[2,10,1]{2,1,0:T(8,128)S(1)}, f32[2,10,1]{2,1,0:T(8,128)S(1)}, u32[]{:S(2)}, u32[]{:S(2)}) collective-permute-start(f32[2,10,1]{2,1,0:T(8,128)S(1)} %get-tuple-element.1087), channel_id=1, source_target_pairs={{0,1},{1,2},{2,3},{3,4},{4,5},{5,6},{6,7},{8,9},{9,10},{10,11},{11... | collective-permute-start | bytes 248 | tf_op jit(solution)/shard_map/ppermute | solution.py:37
  576.2 5.1 collective-permute-start.14
